TPU v7x, 32 devices: a whole 2x2x4 slice. The times are simulated.
32 devices in a mesh: dp: 2 (over x), row: 4 (over y, core), col: 4 (over z).
Axes of the slice: x: 2, y: 2, z: 4, core: 2. Of those that a mesh axis runs over, the one named last changes fastest.
Arguments:
- inputs: bfloat16 [2, 768, 4096], P(None, 'row', ('dp', 'col')), may hold values from -6 to 6
- cotangent: bfloat16 [2, 768, 4096], P(None, 'row', ('dp', 'col')), may hold values from -6 to 6
- lengths: int32 [2, 2], P('dp'), may hold values from 512 to 1536, as said below
- source: int32 [2, 4096], P(None, ('dp', 'col')), may hold values from 0 to 8191, as said below
- query_weight: bfloat16 [768, 768], P('row', 'col'), may hold values from -0.21875 to 0.21875
- key_weight: bfloat16 [768, 768], P('row', 'col'), may hold values from -0.21875 to 0.21875
- value_weight: bfloat16 [768, 768], P('row', 'col'), may hold values from -0.21875 to 0.21875
- output_weight: bfloat16 [768, 768], P('col', 'row'), may hold values from -6 to 6
- inner_weight: bfloat16 [768, 3072], P('row', 'col'), may hold values from -0.21875 to 0.21875
- outer_weight: bfloat16 [768, 3072], P('row', 'col'), may hold values from -0.109375 to 0.109375
- first_gain: float32 [768], P('row'), may hold values from 0.5 to 1.5
- first_shift: float32 [768], P('row'), may hold values from -3 to 3
- second_gain: float32 [768], P('row'), may hold values from 0.5 to 1.5
- second_shift: float32 [768], P('row'), may hold values from -3 to 3
Outputs:
- layer_out: bfloat16 [2, 768, 4096], P(None, 'row', ('dp', 'col'))
- input_grad: bfloat16 [2, 768, 4096], P(None, 'row', ('dp', 'col'))
- query_grad: float32 [768, 768], P('row', 'col')
- key_grad: float32 [768, 768], P('row', 'col')
- value_grad: float32 [768, 768], P('row', 'col')
- output_grad: float32 [768, 768], P('col', 'row')
- inner_grad: float32 [768, 3072], P('row', 'col')
- outer_grad: float32 [768, 3072], P('row', 'col')
- first_gain_grad: float32 [768], P('row')
- first_shift_grad: float32 [768], P('row')
- second_gain_grad: float32 [768], P('row')
- second_shift_grad: float32 [768], P('row')
Inputs may be any that keep to these rules, and one draw needn't show every extreme that they name: lengths is that of each pack's first sequence; the second takes the other 2048 - lengths tokens. source is a permutation of the 8192 flat loader positions, flat index m0 * 2 * 2048 + p0. A token keeps (p // 512) % 4; and for any d, s and col index, exactly 512 of the dealt positions with p // 2048 == d and that col index come from p0 // 2048 == s.
All inputs are finite; a program needn't handle non-finite values.
Results may differ from a plain program's by a relative error of at most 0.018.
Values may be sent and summed in bfloat16 or wider, within the bound.
No kernel may reach another device: no remote copies, remote signals or barrier semaphores. Data moves between devices by JAX's collectives and lax.ppermute only.
A program may use at most 192 MiB of HBM per device.

v0:
```python
import jax
import jax.numpy as jnp
from jax import lax
from jax.sharding import PartitionSpec as P

DH = 64
EPSILON = 1e-05
MASKED_SCORE = -1e30


def rotate(values, positions, rotation_sign):
    row_count, feature = values.shape
    paired = values.reshape(row_count, feature // DH, DH // 2, 2)
    frequency = 10000.0 ** (-2.0 * jnp.arange(DH // 2, dtype=jnp.float32) / DH)
    angles = positions.astype(jnp.float32)[:, None] * frequency[None, :]
    cosine = jnp.cos(angles)[:, None, :]
    sine_part = rotation_sign * jnp.sin(angles)[:, None, :]
    former = paired[..., 0]
    latter = paired[..., 1]
    turned = jnp.stack(
        [former * cosine - latter * sine_part, latter * cosine + former * sine_part], -1
    )
    return turned.reshape(row_count, feature)


def smooth_gate(values):
    return jax.nn.gelu(values, approximate=False)


def contract_last(left, right):
    return lax.dot_general(
        left, right, (((1,), (1,)), ((), ())), preferred_element_type=jnp.float32
    )


def contract_first(left, right):
    return lax.dot_general(
        left, right, (((0,), (0,)), ((), ())), preferred_element_type=jnp.float32
    )


def multiply(row_block, weight, flipped):
    if flipped:
        return contract_last(row_block, weight)
    return jnp.dot(row_block, weight, preferred_element_type=jnp.float32)


def spread_cols(values):
    return lax.all_gather(values, "col", axis=0, tiled=True)


def spread_rows(values):
    return lax.all_gather(values, "row", axis=0, tiled=True)


def reduce_rows(gathered, weight, flipped, share_rows):

    def partial_term(first_row, amount):
        return multiply(gathered, weight, flipped)

    return lax.psum_scatter(
        partial_term(jnp.int32(0), share_rows * lax.axis_size("row")),
        "row",
        scatter_dimension=0,
        tiled=True,
    )


def reduce_cols(gathered, weight, flipped, share_rows):

    def partial_term(first_row, amount):
        return multiply(gathered, weight, flipped)

    return lax.psum_scatter(
        partial_term(jnp.int32(0), share_rows * lax.axis_size("col")),
        "col",
        scatter_dimension=0,
        tiled=True,
    )


def feature_sums(first_sum, second_sum):
    return lax.psum((first_sum, second_sum), "row")


def norm_forward(values, gain, shift):
    feature = values.shape[1] * lax.axis_size("row")
    totals, squares = feature_sums(jnp.sum(values, 1), jnp.sum(values * values, 1))
    centre = totals / feature
    spread = squares / feature - centre * centre
    inverse = lax.rsqrt(spread + EPSILON)
    normed = (values - centre[:, None]) * inverse[:, None]
    return (normed * gain + shift, normed, inverse)


def norm_backward(grad_in, normed, inverse, gain):
    feature = grad_in.shape[1] * lax.axis_size("row")
    scaled = grad_in * gain
    first_sum, second_sum = feature_sums(jnp.sum(scaled, 1), jnp.sum(scaled * normed, 1))
    result = inverse[:, None] * (
        scaled - first_sum[:, None] / feature - normed * second_sum[:, None] / feature
    )
    return (result, jnp.sum(grad_in * normed, 0), jnp.sum(grad_in, 0))


def attend_forward(queries, keyval, same_seq):
    feature = queries.shape[1]
    scaling = DH ** (-0.5)
    results = []
    totals = []
    for head_index in range(feature // DH):
        low_col = head_index * DH
        high_col = low_col + DH
        scores = contract_last(queries[:, low_col:high_col], keyval[:, low_col:high_col]) * scaling
        masked = jnp.where(same_seq, scores, MASKED_SCORE)
        highest = jnp.max(masked, 1, keepdims=True)
        raised = jnp.exp(masked - highest)
        summed = jnp.sum(raised, 1, keepdims=True)
        weights_low = (raised / summed).astype(jnp.bfloat16)
        results.append(
            jnp.dot(
                weights_low,
                keyval[:, feature + low_col : feature + high_col],
                preferred_element_type=jnp.float32,
            )
        )
        totals.append(highest[:, 0] + jnp.log(summed[:, 0]))
    return (jnp.concatenate(results, 1), jnp.stack(totals))


def attend_backward(queries, keyval, grad_attended, totals, same_seq):
    feature = queries.shape[1]
    scaling = DH ** (-0.5)
    grad_queries = []
    grad_keys = []
    grad_values = []
    for head_index in range(feature // DH):
        low_col = head_index * DH
        high_col = low_col + DH
        head_queries = queries[:, low_col:high_col]
        head_keys = keyval[:, low_col:high_col]
        head_values = keyval[:, feature + low_col : feature + high_col]
        head_grad = grad_attended[:, low_col:high_col]
        scores = contract_last(head_queries, head_keys) * scaling
        masked = jnp.where(same_seq, scores, MASKED_SCORE)
        weights_full = jnp.exp(masked - totals[head_index][:, None])
        grad_weights = contract_last(head_grad, head_values)
        centre = jnp.sum(weights_full * grad_weights, 1, keepdims=True)
        grad_scores = (weights_full * (grad_weights - centre)).astype(jnp.bfloat16)
        grad_queries.append(
            jnp.dot(grad_scores, head_keys, preferred_element_type=jnp.float32) * scaling
        )
        grad_keys.append(contract_first(grad_scores, head_queries) * scaling)
        grad_values.append(contract_first(weights_full.astype(jnp.bfloat16), head_grad))
    return (jnp.concatenate(grad_queries, 1), jnp.concatenate(grad_keys + grad_values, 1))


def body(
    inputs,
    cotangent,
    lengths,
    source,
    query_weight,
    key_weight,
    value_weight,
    output_weight,
    inner_weight,
    outer_weight,
    first_gain,
    first_shift,
    second_gain,
    second_shift,
):
    micro, local_width, share_rows = inputs.shape
    dp_count = lax.axis_size("dp")
    pack_rows = share_rows * lax.axis_size("col")
    local_count = micro * share_rows
    sent_rows = local_count // dp_count
    anchor = source.reshape(local_count)
    anchor_pack = anchor % (dp_count * pack_rows)
    sender = anchor_pack // pack_rows
    wanted = anchor // (dp_count * pack_rows) * share_rows + anchor_pack % share_rows
    order = jnp.argsort(sender, stable=True)
    requested = lax.all_to_all(
        wanted[order].reshape(dp_count, sent_rows), "dp", split_axis=0, concat_axis=0, tiled=True
    )
    asked = requested.reshape(local_count)
    flat_in = inputs.transpose(0, 2, 1).reshape(local_count, local_width)
    flat_cot = cotangent.transpose(0, 2, 1).reshape(local_count, local_width)
    arrived_in, arrived_cot = (
        lax.all_to_all(flat_in[asked], "dp", split_axis=0, concat_axis=0, tiled=True),
        lax.all_to_all(flat_cot[asked], "dp", split_axis=0, concat_axis=0, tiled=True),
    )
    placing = jnp.argsort(order)
    dealt_in = arrived_in[placing]
    dealt_cot = arrived_cot[placing]
    head_width = query_weight.shape[1]
    qkv_weight = jnp.concatenate([query_weight, key_weight, value_weight], 1)
    own_pos = lax.axis_index("row") * share_rows + jnp.arange(share_rows, dtype=jnp.int32)
    all_pos = jnp.arange(pack_rows, dtype=jnp.int32)
    grad_qkv = jnp.zeros(qkv_weight.shape, jnp.float32)
    grad_output = jnp.zeros(output_weight.shape, jnp.float32)
    grad_inner = jnp.zeros(inner_weight.shape, jnp.float32)
    grad_outer = jnp.zeros(outer_weight.shape, jnp.float32)
    gain_one = jnp.zeros(first_gain.shape, jnp.float32)
    shift_one = jnp.zeros(first_gain.shape, jnp.float32)
    gain_two = jnp.zeros(first_gain.shape, jnp.float32)
    shift_two = jnp.zeros(first_gain.shape, jnp.float32)
    output_rows = []
    grad_rows = []
    for step_index in range(micro):
        boundary = lengths[0, step_index]
        own_side = own_pos >= boundary
        all_side = all_pos >= boundary
        own_place = own_pos - jnp.where(own_side, boundary, 0)
        block_in = dealt_in[step_index * share_rows : (step_index + 1) * share_rows]
        block_cot = dealt_cot[step_index * share_rows : (step_index + 1) * share_rows]
        tokens_full = spread_cols(block_in)
        projected = reduce_rows(tokens_full, qkv_weight, False, share_rows)
        queries = rotate(projected[:, :head_width], own_place, 1.0).astype(jnp.bfloat16)
        own_keys = rotate(projected[:, head_width : 2 * head_width], own_place, 1.0)
        own_kv = jnp.concatenate([own_keys, projected[:, 2 * head_width :]], 1).astype(jnp.bfloat16)
        keyval = spread_rows(own_kv)
        same_seq = own_side[:, None] == all_side[None, :]
        attended, log_totals = attend_forward(queries, keyval, same_seq)
        attended_full = spread_rows(attended.astype(jnp.bfloat16))
        branch = reduce_cols(attended_full, output_weight, False, share_rows)
        hidden, first_normed, first_inverse = norm_forward(
            block_in.astype(jnp.float32) + branch, first_gain, first_shift
        )
        hidden_full = spread_cols(hidden.astype(jnp.bfloat16))
        inner = reduce_rows(hidden_full, inner_weight, False, share_rows)
        activated_full = spread_rows(smooth_gate(inner).astype(jnp.bfloat16))
        outer = reduce_cols(activated_full, outer_weight, True, share_rows)
        result, second_normed, second_inverse = norm_forward(
            hidden + outer, second_gain, second_shift
        )
        output_rows.append(result.astype(jnp.bfloat16))
        grad_second, gain_piece, shift_piece = norm_backward(
            block_cot.astype(jnp.float32), second_normed, second_inverse, second_gain
        )
        gain_two = gain_two + gain_piece
        shift_two = shift_two + shift_piece
        outer_full = spread_cols(grad_second.astype(jnp.bfloat16))
        grad_outer = grad_outer + contract_first(outer_full, activated_full)
        grad_act = reduce_rows(outer_full, outer_weight, False, share_rows)
        inner_low = jax.vjp(smooth_gate, inner)[1](grad_act)[0].astype(jnp.bfloat16)
        inner_full = spread_rows(inner_low)
        grad_inner = grad_inner + contract_first(hidden_full, inner_full)
        grad_hidden = grad_second + reduce_cols(inner_full, inner_weight, True, share_rows)
        grad_first, gain_piece, shift_piece = norm_backward(
            grad_hidden, first_normed, first_inverse, first_gain
        )
        gain_one = gain_one + gain_piece
        shift_one = shift_one + shift_piece
        branch_full = spread_cols(grad_first.astype(jnp.bfloat16))
        grad_output = grad_output + contract_first(attended_full, branch_full)
        grad_attended = reduce_rows(branch_full, output_weight, True, share_rows).astype(
            jnp.bfloat16
        )
        grad_query, grad_keyval = attend_backward(
            queries, keyval, grad_attended, log_totals, same_seq
        )
        keyval_share = lax.psum_scatter(
            grad_keyval.astype(jnp.bfloat16), "row", scatter_dimension=0, tiled=True
        ).astype(jnp.float32)
        own_low = jnp.concatenate(
            [
                rotate(grad_query, own_place, -1.0),
                rotate(keyval_share[:, :head_width], own_place, -1.0),
                keyval_share[:, head_width:],
            ],
            1,
        ).astype(jnp.bfloat16)
        grads_full = spread_rows(own_low)
        grad_qkv = grad_qkv + contract_first(tokens_full, grads_full)
        grad_tokens = grad_first + reduce_cols(grads_full, qkv_weight, True, share_rows)
        grad_rows.append(grad_tokens.astype(jnp.bfloat16))
    summed_qkv, summed_output, summed_inner, summed_outer = (
        lax.psum(grad_qkv.astype(jnp.bfloat16), "dp").astype(jnp.float32),
        lax.psum(grad_output.astype(jnp.bfloat16), "dp").astype(jnp.float32),
        lax.psum(grad_inner.astype(jnp.bfloat16), "dp").astype(jnp.float32),
        lax.psum(grad_outer.astype(jnp.bfloat16), "dp").astype(jnp.float32),
    )
    gain_one, shift_one, gain_two, shift_two = lax.psum(
        (gain_one, shift_one, gain_two, shift_two), ("dp", "col")
    )
    results_all = jnp.concatenate(output_rows, 0)
    grads_all = jnp.concatenate(grad_rows, 0)
    returned_out, returned_grad = (
        lax.all_to_all(results_all[order], "dp", split_axis=0, concat_axis=0, tiled=True),
        lax.all_to_all(grads_all[order], "dp", split_axis=0, concat_axis=0, tiled=True),
    )
    restore = jnp.argsort(asked)
    final_out = returned_out[restore].reshape(micro, share_rows, local_width).transpose(0, 2, 1)
    final_grad = returned_grad[restore].reshape(micro, share_rows, local_width).transpose(0, 2, 1)
    return (
        final_out,
        final_grad,
        summed_qkv[:, :head_width],
        summed_qkv[:, head_width : 2 * head_width],
        summed_qkv[:, 2 * head_width :],
        summed_output,
        summed_inner,
        summed_outer,
        gain_one,
        shift_one,
        gain_two,
        shift_two,
    )


def solution(mesh):
    return jax.shard_map(
        body,
        mesh=mesh,
        in_specs=(
            P(None, "row", ("dp", "col")),
            P(None, "row", ("dp", "col")),
            P("dp", None),
            P(None, ("dp", "col")),
            P("row", "col"),
            P("row", "col"),
            P("row", "col"),
            P("col", "row"),
            P("row", "col"),
            P("row", "col"),
            P("row"),
            P("row"),
            P("row"),
            P("row"),
        ),
        out_specs=(
            P(None, "row", ("dp", "col")),
            P(None, "row", ("dp", "col")),
            P("row", "col"),
            P("row", "col"),
            P("row", "col"),
            P("col", "row"),
            P("row", "col"),
            P("row", "col"),
            P("row"),
            P("row"),
            P("row"),
            P("row"),
        ),
        check_vma=False,
    )
```

profile of v0, /device:TPU:0, one launch (start us, length us, event | category | flops | bytes accessed | tf_op | source)
XLA Modules:
  0.0 1247.9 jit_solution(11385265382036397583)
XLA Ops:
  8.0 4.4 sort.48
  12.3 8.8 gather_fusion
  25.4 4.4 sort.49
  39.0 7.0 all-to-all-done.1
  50.4 20.3 %all_gather.54 = bf16[2048,192]{0,1:T(8,128)(2,1)S(1)} all-gather(bf16[512,192]{0,1:T(8,128)(2,1)S(1)} %copy.64), channel_id=1, replica_groups=mesh['dp'=2,'row'=4,'col'=4] {'col'}, dimensions={0}, use_global_device_ids=true | all-gather | bytes 983040 | tf_op jit(solution)/shard_map/all_gather | solution.py:49
  74.9 17.7 %all_gather.59 = bf16[2048,192]{0,1:T(8,128)(2,1)S(1)} all-gather(bf16[512,192]{0,1:T(8,128)(2,1)S(1)} %copy.65), channel_id=1, replica_groups=mesh['dp'=2,'row'=4,'col'=4] {'col'}, dimensions={0}, use_global_device_ids=true | all-gather | bytes 983040 | tf_op jit(solution)/shard_map/all_gather | solution.py:49
  100.4 20.8 %reduce-scatter.19.cloned.1.call-done = f32[512,576]{0,1:T(8,128)} async-done(((f32[2048,576]{0,1:T(8,128)}), f32[512,576]{0,1:T(8,128)}) %reduce-scatter.19.cloned.1.call-update) | async-done | bytes 1179664 | tf_op jit(solution)/shard_map/reduce_scatter | solution.py:61
  129.5 42.3 %reduce-scatter.27.cloned.1.call-done = f32[512,576]{0,1:T(8,128)} async-done(((f32[2048,576]{0,1:T(8,128)}), f32[512,576]{0,1:T(8,128)}) %reduce-scatter.27.cloned.1.call-update) | async-done | bytes 1179664 | tf_op jit(solution)/shard_map/reduce_scatter | solution.py:61
  177.6 16.0 %all-gather.9.cloned.1.call-done = bf16[2048,384]{0,1:T(8,128)(2,1)} async-done(((bf16[512,384]{0,1:T(8,128)(2,1)}), bf16[2048,384]{0,1:T(8,128)(2,1)}) %all-gather.9.cloned.1.call-update) | async-done | bytes 1572880 | tf_op jit(solution)/shard_map/all_gather | solution.py:53
  204.4 13.3 %all_gather.56 = bf16[2048,192]{0,1:T(8,128)(2,1)S(1)} all-gather(bf16[512,192]{0,1:T(8,128)(2,1)S(1)} %pad_maximum_fusion.11), channel_id=1, replica_groups=mesh['dp'=2,'row'=4,'col'=4] {'row'}, dimensions={0}, use_global_device_ids=true | all-gather | bytes 983040 | tf_op jit(solution)/shard_map/all_gather | solution.py:53
  231.2 8.7 all_gather.61
  242.5 14.5 %reduce-scatter.21.cloned.1.call-done = f32[512,192]{0,1:T(8,128)} async-done(((f32[2048,192]{0,1:T(8,128)}), f32[512,192]{0,1:T(8,128)}) %reduce-scatter.21.cloned.1.call-update) | async-done | bytes 393232 | tf_op jit(solution)/shard_map/reduce_scatter | solution.py:74
  258.1 35.4 %reduce-scatter.29.cloned.1.call-done = f32[512,192]{0,1:T(8,128)} async-done(((f32[2048,192]{0,1:T(8,128)}), f32[512,192]{0,1:T(8,128)}) %reduce-scatter.29.cloned.1.call-update) | async-done | bytes 393232 | tf_op jit(solution)/shard_map/reduce_scatter | solution.py:74
  294.6 6.5 all-reduce.4
  301.3 18.0 %all_gather.57 = bf16[2048,192]{0,1:T(8,128)(2,1)S(1)} all-gather(bf16[512,192]{0,1:T(8,128)(2,1)S(1)} %fusion.85), channel_id=1, replica_groups=mesh['dp'=2,'row'=4,'col'=4] {'col'}, dimensions={0}, use_global_device_ids=true | all-gather | bytes 983040 | tf_op jit(solution)/shard_map/all_gather | solution.py:49
  323.9 57.5 %reduce-scatter.23.cloned.1.call-done = f32[512,768]{1,0:T(8,128)} async-done(((f32[2048,768]{1,0:T(8,128)}), f32[512,768]{1,0:T(8,128)}) %reduce-scatter.23.cloned.1.call-update) | async-done | bytes 1572880 | tf_op jit(solution)/shard_map/reduce_scatter | solution.py:61
  381.4 5.5 multiply_convert_fusion.7
  387.0 28.6 %all-gather.11.cloned.1.call-done = bf16[2048,768]{1,0:T(8,128)(2,1)} async-done(((bf16[512,768]{1,0:T(8,128)(2,1)}), bf16[2048,768]{1,0:T(8,128)(2,1)}) %all-gather.11.cloned.1.call-update) | async-done | bytes 3145744 | tf_op jit(solution)/shard_map/all_gather | solution.py:53
  415.7 4.3 fusion.186
  420.0 35.4 %reduce-scatter.25.cloned.1.call-done = f32[512,192]{0,1:T(8,128)} async-done(((f32[2048,192]{0,1:T(8,128)}), f32[512,192]{0,1:T(8,128)}) %reduce-scatter.25.cloned.1.call-update) | async-done | bytes 393232 | tf_op jit(solution)/shard_map/reduce_scatter | solution.py:74
  456.6 18.6 %all_gather.62 = bf16[2048,192]{0,1:T(8,128)(2,1)S(1)} all-gather(bf16[512,192]{0,1:T(8,128)(2,1)S(1)} %get-tuple-element.129), channel_id=1, replica_groups=mesh['dp'=2,'row'=4,'col'=4] {'col'}, dimensions={0}, use_global_device_ids=true | all-gather | bytes 983040 | tf_op jit(solution)/shard_map/all_gather | solution.py:49
  479.9 57.8 %reduce-scatter.31.cloned.1.call-done = f32[512,768]{1,0:T(8,128)} async-done(((f32[2048,768]{1,0:T(8,128)}), f32[512,768]{1,0:T(8,128)}) %reduce-scatter.31.cloned.1.call-update) | async-done | bytes 1572880 | tf_op jit(solution)/shard_map/reduce_scatter | solution.py:61
  537.6 5.5 multiply_convert_fusion.6
  543.2 28.6 %all-gather.15.cloned.1.call-done = bf16[2048,768]{1,0:T(8,128)(2,1)} async-done(((bf16[512,768]{1,0:T(8,128)(2,1)}), bf16[2048,768]{1,0:T(8,128)(2,1)}) %all-gather.15.cloned.1.call-update) | async-done | bytes 3145744 | tf_op jit(solution)/shard_map/all_gather | solution.py:53
  581.4 9.7 all_to_all.57
  595.5 16.0 %reduce-scatter.33.cloned.1.call-done = f32[512,192]{0,1:T(8,128)} async-done(((f32[2048,192]{0,1:T(8,128)}), f32[512,192]{0,1:T(8,128)}) %reduce-scatter.33.cloned.1.call-update) | async-done | bytes 393232 | tf_op jit(solution)/shard_map/reduce_scatter | solution.py:74
  612.7 6.5 all-reduce.3
  620.2 5.9 all-reduce.2
  626.4 18.0 %all_gather.68 = bf16[2048,192]{0,1:T(8,128)(2,1)S(1)} all-gather(bf16[512,192]{0,1:T(8,128)(2,1)S(1)} %get-tuple-element.139), channel_id=1, replica_groups=mesh['dp'=2,'row'=4,'col'=4] {'col'}, dimensions={0}, use_global_device_ids=true | all-gather | bytes 983040 | tf_op jit(solution)/shard_map/all_gather | solution.py:49
  649.1 17.4 %all_gather.64 = bf16[2048,192]{0,1:T(8,128)(2,1)S(1)} all-gather(bf16[512,192]{0,1:T(8,128)(2,1)S(1)} %get-tuple-element.138), channel_id=1, replica_groups=mesh['dp'=2,'row'=4,'col'=4] {'col'}, dimensions={0}, use_global_device_ids=true | all-gather | bytes 983040 | tf_op jit(solution)/shard_map/all_gather | solution.py:49
  671.3 35.0 %reduce-scatter.45.cloned.1.call-done = f32[512,768]{1,0:T(8,128)} async-done(((f32[2048,768]{1,0:T(8,128)}), f32[512,768]{1,0:T(8,128)}) %reduce-scatter.45.cloned.1.call-update) | async-done | bytes 1572880 | tf_op jit(solution)/shard_map/reduce_scatter | solution.py:61
  710.2 57.0 %reduce-scatter.35.cloned.1.call-done = f32[512,768]{1,0:T(8,128)} async-done(((f32[2048,768]{1,0:T(8,128)}), f32[512,768]{1,0:T(8,128)}) %reduce-scatter.35.cloned.1.call-update) | async-done | bytes 1572880 | tf_op jit(solution)/shard_map/reduce_scatter | solution.py:61
  771.2 26.0 %all-gather.21.cloned.1.call-done = bf16[2048,768]{1,0:T(8,128)(2,1)} async-done(((bf16[512,768]{1,0:T(8,128)(2,1)}), bf16[2048,768]{1,0:T(8,128)(2,1)}) %all-gather.21.cloned.1.call-update) | async-done | bytes 3145744 | tf_op jit(solution)/shard_map/all_gather | solution.py:53
  801.5 25.7 %all-gather.17.cloned.1.call-done = bf16[2048,768]{1,0:T(8,128)(2,1)} async-done(((bf16[512,768]{1,0:T(8,128)(2,1)}), bf16[2048,768]{1,0:T(8,128)(2,1)}) %all-gather.17.cloned.1.call-update) | async-done | bytes 3145744 | tf_op jit(solution)/shard_map/all_gather | solution.py:53
  831.7 33.0 %reduce-scatter.47.cloned.1.call-done = f32[512,192]{0,1:T(8,128)} async-done(((f32[2048,192]{0,1:T(8,128)}), f32[512,192]{0,1:T(8,128)}) %reduce-scatter.47.cloned.1.call-update) | async-done | bytes 393232 | tf_op jit(solution)/shard_map/reduce_scatter | solution.py:74
  866.7 34.4 %reduce-scatter.37.cloned.1.call-done = f32[512,192]{0,1:T(8,128)} async-done(((f32[2048,192]{0,1:T(8,128)}), f32[512,192]{0,1:T(8,128)}) %reduce-scatter.37.cloned.1.call-update) | async-done | bytes 393232 | tf_op jit(solution)/shard_map/reduce_scatter | solution.py:74
  903.7 6.5 all-reduce.1
  910.5 18.0 %all_gather.66 = bf16[2048,192]{0,1:T(8,128)(2,1)S(1)} all-gather(bf16[512,192]{0,1:T(8,128)(2,1)S(1)} %get-tuple-element.136), channel_id=1, replica_groups=mesh['dp'=2,'row'=4,'col'=4] {'col'}, dimensions={0}, use_global_device_ids=true | all-gather | bytes 983040 | tf_op jit(solution)/shard_map/all_gather | solution.py:49
  931.1 17.3 %all_gather.70 = bf16[2048,192]{0,1:T(8,128)(2,1)S(1)} all-gather(bf16[512,192]{0,1:T(8,128)(2,1)S(1)} %get-tuple-element.137), channel_id=1, replica_groups=mesh['dp'=2,'row'=4,'col'=4] {'col'}, dimensions={0}, use_global_device_ids=true | all-gather | bytes 983040 | tf_op jit(solution)/shard_map/all_gather | solution.py:49
  950.9 7.3 reduce-scatter.39.cloned.1.call-done
  976.6 12.3 reduce-scatter.49.cloned.1.call-done
  1033.9 16.7 %reduce-scatter.51.cloned.1.call-done = bf16[512,384]{0,1:T(8,128)(2,1)} async-done(((bf16[2048,384]{0,1:T(8,128)(2,1)}), bf16[512,384]{0,1:T(8,128)(2,1)}) %reduce-scatter.51.cloned.1.call-update) | async-done | bytes 393232 | tf_op jit(solution)/shard_map/reduce_scatter | solution.py:264
  1079.6 23.4 %all-gather.23.cloned.1.call-done = bf16[2048,576]{0,1:T(8,128)(2,1)} async-done(((bf16[512,576]{0,1:T(8,128)(2,1)}), bf16[2048,576]{0,1:T(8,128)(2,1)}) %all-gather.23.cloned.1.call-update) | async-done | bytes 2359312 | tf_op jit(solution)/shard_map/all_gather | solution.py:53
  1113.1 4.4 sort.50
  1126.3 22.8 %all-reduce = (f32[192]{0:T(256)}, f32[192]{0:T(256)}, f32[192]{0:T(256)}, f32[192]{0:T(256)}) all-reduce(f32[192]{0:T(256)S(1)} %add.349, f32[192]{0:T(256)S(1)} %add.350, f32[192]{0:T(256)S(1)} %add.351, f32[192]{0:T(256)S(1)} %add.352), channel_id=1, replica_groups=mesh['dp'=2,'row'=4,'col'=4] {'dp','col'}, use_global_device_ids=true, to_apply=%region_77.78 | all-reduce | flops 768 | bytes 6144 | tf_op jit(solution)/shard_map/psum | solution.py:285
  1159.5 23.1 %reduce-scatter.43.cloned.1.call-done = f32[512,192]{0,1:T(8,128)} async-done(((f32[2048,192]{0,1:T(8,128)}), f32[512,192]{0,1:T(8,128)}) %reduce-scatter.43.cloned.1.call-update) | async-done | bytes 393232 | tf_op jit(solution)/shard_map/reduce_scatter | solution.py:74
  1182.5 36.5 %reduce-scatter.53.cloned.1.call-done = f32[512,192]{0,1:T(8,128)} async-done(((f32[2048,192]{0,1:T(8,128)}), f32[512,192]{0,1:T(8,128)}) %reduce-scatter.53.cloned.1.call-update) | async-done | bytes 393232 | tf_op jit(solution)/shard_map/reduce_scatter | solution.py:74
  1230.0 5.8 all-to-all-done.4
  (448 shorter events, 273.2 us)
Async XLA Ops:
  7.2 408.5 %copy-start = (bf16[192,768]{1,0:T(8,128)(2,1)S(1)}, bf16[192,768]{1,0:T(8,128)(2,1)}, u32[]{:S(2)}) copy-start(bf16[192,768]{1,0:T(8,128)(2,1)} %param.23) | copy-start | bytes 884740
  21.2 8.8 all-to-all-start
  35.5 10.5 all-to-all-start.1
  38.9 82.2 %reduce-scatter.19.cloned.1.call-start = ((), (), s32[]{:S(2)}) async-start(), calls=%async_computation.23 | async-start | bytes 5898240 | tf_op jit(solution)/shard_map/reduce_scatter | solution.py:61
  74.8 97.0 %reduce-scatter.27.cloned.1.call-start = ((), (), s32[]{:S(2)}) async-start(), calls=%async_computation.29 | async-start | bytes 5898240 | tf_op jit(solution)/shard_map/reduce_scatter | solution.py:61
  96.7 96.9 %all-gather.9.cloned.1.call-start = ((), (), s32[]{:S(2)}) async-start(), calls=%async_computation.24 | async-start | bytes 1966080 | tf_op jit(solution)/shard_map/all_gather | solution.py:53
  126.2 94.2 %all-gather.13.cloned.1.call-start = ((), (), s32[]{:S(2)}) async-start(), calls=%async_computation.30 | async-start | bytes 1966080 | tf_op jit(solution)/shard_map/all_gather | solution.py:53
  129.5 69.4 %copy-start.69 = (bf16[512,192]{0,1:T(8,128)(2,1)}, bf16[512,192]{0,1:T(8,128)(2,1)S(1)}, u32[]{:S(2)}) copy-start(bf16[512,192]{0,1:T(8,128)(2,1)S(1)} %convert_element_type.178) | copy-start | bytes 589828
  175.0 50.7 %copy-start.67 = (bf16[512,192]{0,1:T(8,128)(2,1)}, bf16[512,192]{0,1:T(8,128)(2,1)S(1)}, u32[]{:S(2)}) copy-start(bf16[512,192]{0,1:T(8,128)(2,1)S(1)} %convert_element_type.187) | copy-start | bytes 589828
  177.4 79.7 %reduce-scatter.21.cloned.1.call-start = ((), (), s32[]{:S(2)}) async-start(), calls=%async_computation.25 | async-start | bytes 1966080 | tf_op jit(solution)/shard_map/reduce_scatter | solution.py:74
  220.2 73.3 %reduce-scatter.29.cloned.1.call-start = ((), (), s32[]{:S(2)}) async-start(), calls=%async_computation.31 | async-start | bytes 1966080 | tf_op jit(solution)/shard_map/reduce_scatter | solution.py:74
  242.4 58.7 %copy-start.81 = (f32[192]{0:T(256)S(1)}, f32[192]{0:T(256)}, u32[]{:S(2)}) copy-start(f32[192]{0:T(256)} %param.24) | copy-start | bytes 2308
  242.4 58.7 %copy-start.85 = (f32[192]{0:T(256)S(1)}, f32[192]{0:T(256)}, u32[]{:S(2)}) copy-start(f32[192]{0:T(256)} %param.25) | copy-start | bytes 2308
  242.5 77.7 %copy-start.50 = (bf16[192,768]{1,0:T(8,128)(2,1)S(1)}, bf16[192,768]{1,0:T(8,128)(2,1)}, u32[]{:S(2)}) copy-start(bf16[192,768]{1,0:T(8,128)(2,1)} %param.22) | copy-start | bytes 884740
  242.5 139.0 %reduce-scatter.23.cloned.1.call-start = ((), (), s32[]{:S(2)}) async-start(), calls=%async_computation.26 | async-start | bytes 7864320 | tf_op jit(solution)/shard_map/reduce_scatter | solution.py:61
  258.1 652.1 %copy-start.26 = (f32[512,192]{0,1:T(8,128)}, f32[512,192]{0,1:T(8,128)S(1)}, u32[]{:S(2)}) copy-start(f32[512,192]{0,1:T(8,128)S(1)} %get-tuple-element.74) | copy-start | bytes 1179652
  294.6 615.6 %copy-start.28 = (f32[512,192]{0,1:T(8,128)}, f32[512,192]{0,1:T(8,128)S(1)}, u32[]{:S(2)}) copy-start(f32[512,192]{0,1:T(8,128)S(1)} %get-tuple-element.75) | copy-start | bytes 1179652
  323.9 91.8 %all-gather.11.cloned.1.call-start = ((), (), s32[]{:S(2)}) async-start(), calls=%async_computation.27 | async-start | bytes 3932160 | tf_op jit(solution)/shard_map/all_gather | solution.py:53
  387.0 68.4 %reduce-scatter.25.cloned.1.call-start = ((), (), s32[]{:S(2)}) async-start(), calls=%async_computation.28 | async-start | bytes 1966080 | tf_op jit(solution)/shard_map/reduce_scatter | solution.py:74
  420.0 117.6 %reduce-scatter.31.cloned.1.call-start = ((), (), s32[]{:S(2)}) async-start(), calls=%async_computation.32 | async-start | bytes 7864320 | tf_op jit(solution)/shard_map/reduce_scatter | solution.py:61
  479.8 92.0 %all-gather.15.cloned.1.call-start = ((), (), s32[]{:S(2)}) async-start(), calls=%async_computation.33 | async-start | bytes 3932160 | tf_op jit(solution)/shard_map/all_gather | solution.py:53
  543.2 68.3 %reduce-scatter.33.cloned.1.call-start = ((), (), s32[]{:S(2)}) async-start(), calls=%async_computation.34 | async-start | bytes 1966080 | tf_op jit(solution)/shard_map/reduce_scatter | solution.py:74
  576.1 130.2 %reduce-scatter.45.cloned.1.call-start = ((), (), s32[]{:S(2)}) async-start(), calls=%async_computation.42 | async-start | bytes 7864320 | tf_op jit(solution)/shard_map/reduce_scatter | solution.py:61
  649.0 118.2 %reduce-scatter.35.cloned.1.call-start = ((), (), s32[]{:S(2)}) async-start(), calls=%async_computation.35 | async-start | bytes 7864320 | tf_op jit(solution)/shard_map/reduce_scatter | solution.py:61
  671.3 125.9 %all-gather.21.cloned.1.call-start = ((), (), s32[]{:S(2)}) async-start(), calls=%async_computation.43 | async-start | bytes 3932160 | tf_op jit(solution)/shard_map/all_gather | solution.py:53
  710.2 117.0 %all-gather.17.cloned.1.call-start = ((), (), s32[]{:S(2)}) async-start(), calls=%async_computation.36 | async-start | bytes 3932160 | tf_op jit(solution)/shard_map/all_gather | solution.py:53
  771.2 93.5 %reduce-scatter.47.cloned.1.call-start = ((), (), s32[]{:S(2)}) async-start(), calls=%async_computation.44 | async-start | bytes 1966080 | tf_op jit(solution)/shard_map/reduce_scatter | solution.py:74
  801.4 99.7 %reduce-scatter.37.cloned.1.call-start = ((), (), s32[]{:S(2)}) async-start(), calls=%async_computation.37 | async-start | bytes 1966080 | tf_op jit(solution)/shard_map/reduce_scatter | solution.py:74
  831.4 33.3 %copy-start.86 = (f32[192]{0:T(256)S(1)}, f32[192]{0:T(256)}, u32[]{:S(2)}) copy-start(f32[192]{0:T(256)} %param.27) | copy-start | bytes 2308
  831.4 126.8 %reduce-scatter.39.cloned.1.call-start = ((), (), s32[]{:S(2)}) async-start(), calls=%async_computation.38 | async-start | bytes 1966080 | tf_op jit(solution)/shard_map/reduce_scatter | solution.py:61
  866.7 43.8 %copy-start.51 = (f32[512,192]{0,1:T(8,128)}, f32[512,192]{0,1:T(8,128)S(1)}, u32[]{:S(2)}) copy-start(f32[512,192]{0,1:T(8,128)S(1)} %get-tuple-element.67) | copy-start | bytes 1179652
  903.7 27.2 %copy-start.53 = (f32[512,192]{0,1:T(8,128)}, f32[512,192]{0,1:T(8,128)S(1)}, u32[]{:S(2)}) copy-start(f32[512,192]{0,1:T(8,128)S(1)} %get-tuple-element.66) | copy-start | bytes 1179652
  931.0 58.0 %reduce-scatter.49.cloned.1.call-start = ((), (), s32[]{:S(2)}) async-start(), calls=%async_computation.45 | async-start | bytes 1966080 | tf_op jit(solution)/shard_map/reduce_scatter | solution.py:61
  950.9 68.9 %reduce-scatter.41.cloned.1.call-start = ((), (), s32[]{:S(2)}) async-start(), calls=%async_computation.39 | async-start | bytes 1966080 | tf_op jit(solution)/shard_map/reduce_scatter | solution.py:264
  976.4 74.3 %reduce-scatter.51.cloned.1.call-start = ((), (), s32[]{:S(2)}) async-start(), calls=%async_computation.46 | async-start | bytes 1966080 | tf_op jit(solution)/shard_map/reduce_scatter | solution.py:264
  1011.0 65.9 %all-gather.19.cloned.1.call-start = ((), (), s32[]{:S(2)}) async-start(), calls=%async_computation.40 | async-start | bytes 2949120 | tf_op jit(solution)/shard_map/all_gather | solution.py:53
  1027.7 75.3 %all-gather.23.cloned.1.call-start = ((), (), s32[]{:S(2)}) async-start(), calls=%async_computation.47 | async-start | bytes 2949120 | tf_op jit(solution)/shard_map/all_gather | solution.py:53
  1062.5 91.8 %all-reduce.8.cloned.1.call-start = ((), (), s32[]{:S(2)}) async-start(), calls=%async_computation.49 | async-start | bytes 1867776 | tf_op jit(solution)/shard_map/psum | solution.py:280
  1073.1 29.9 %copy-start.33 = (bf16[2048,192]{0,1:T(8,128)(2,1)S(1)}, bf16[2048,192]{0,1:T(8,128)(2,1)}, u32[]{:S(2)}) copy-start(bf16[2048,192]{0,1:T(8,128)(2,1)} %copy-done.32) | copy-start | bytes 2359300
  1079.6 26.9 %copy-start.58 = (bf16[192,192]{1,0:T(8,128)(2,1)S(1)}, bf16[192,192]{1,0:T(8,128)(2,1)}, u32[]{:S(2)}) copy-start(bf16[192,192]{1,0:T(8,128)(2,1)} %param.20) | copy-start | bytes 221188
  1106.4 76.1 %reduce-scatter.43.cloned.1.call-start = ((), (), s32[]{:S(2)}) async-start(), calls=%async_computation.41 | async-start | bytes 1966080 | tf_op jit(solution)/shard_map/reduce_scatter | solution.py:74
  1110.4 108.7 %reduce-scatter.53.cloned.1.call-start = ((), (), s32[]{:S(2)}) async-start(), calls=%async_computation.48 | async-start | bytes 1966080 | tf_op jit(solution)/shard_map/reduce_scatter | solution.py:74
  1122.7 26.4 %all-to-all-start.2 = ((bf16[2,512,192]{1,2,0:T(8,128)(2,1)}), bf16[2,512,192]{1,2,0:T(8,128)(2,1)S(1)}, u32[]{:S(2)}, u32[]{:S(2)}) async-start(bf16[2,512,192]{1,2,0:T(8,128)(2,1)} %copy.52), calls=%async_computation.10 | async-start | bytes 786432 | tf_op jit(solution)/shard_map/all_to_all | solution.py:291
  1153.3 65.8 %copy-start.27 = (f32[512,192]{0,1:T(8,128)S(1)}, f32[512,192]{0,1:T(8,128)}, u32[]{:S(2)}) copy-start(f32[512,192]{0,1:T(8,128)} %copy-done.26) | copy-start | bytes 1179652
  1153.3 65.8 %copy-start.29 = (f32[512,192]{0,1:T(8,128)S(1)}, f32[512,192]{0,1:T(8,128)}, u32[]{:S(2)}) copy-start(f32[512,192]{0,1:T(8,128)} %copy-done.28) | copy-start | bytes 1179652
  1153.3 65.8 %copy-start.52 = (f32[512,192]{0,1:T(8,128)S(1)}, f32[512,192]{0,1:T(8,128)}, u32[]{:S(2)}) copy-start(f32[512,192]{0,1:T(8,128)} %copy-done.51) | copy-start | bytes 1179652
  1153.3 65.8 %copy-start.54 = (f32[512,192]{0,1:T(8,128)S(1)}, f32[512,192]{0,1:T(8,128)}, u32[]{:S(2)}) copy-start(f32[512,192]{0,1:T(8,128)} %copy-done.53) | copy-start | bytes 1179652
  1225.6 10.2 all-to-all-start.4
  (76 other events, 403.7 us)
Sparse Core Ops, SparseCore 0:
  74.9 46.2 reduce-scatter.18
  123.9 47.8 reduce-scatter.26
  173.9 19.6 all-gather.8
  195.6 23.8 all-gather.12
  221.6 35.3 reduce-scatter.20
  259.2 34.2 reduce-scatter.28
  324.0 57.3 reduce-scatter.22
  387.1 28.5 all-gather.10
  420.1 35.2 reduce-scatter.24
  479.9 57.6 reduce-scatter.30
  543.3 28.5 all-gather.14
  576.2 35.2 reduce-scatter.32
  649.1 57.0 reduce-scatter.44
  708.8 58.3 reduce-scatter.34
  768.6 28.5 all-gather.20
  798.6 28.5 all-gather.16
  829.3 35.2 reduce-scatter.46
  866.8 34.2 reduce-scatter.36
  931.1 27.1 reduce-scatter.38
  960.8 28.1 reduce-scatter.48
  991.5 28.1 reduce-scatter.40
  1022.4 28.1 reduce-scatter.50
  1052.8 24.0 all-gather.18
  1078.9 24.0 all-gather.22
  1106.6 38.2 all-reduce.7
  1147.1 35.3 reduce-scatter.42
  1184.8 34.2 reduce-scatter.52
where the time goes:
time: 1260 us; the launch traced here: 1250 us
  waiting for transfers between devices  702 us (56%)
  blocking collectives  225 us (18%)
  matrix products  114 us (9%)
  other arithmetic  87.5 us (7%)
  local copies, waits for them, and re-layouts  85.6 us (7%)
  starting transfers between devices  17.1 us (1%)
  between operations  16.2 us (1%)
    reduce_scatter x8, waiting for transfers between devices, reduce_rows(): lax.psum_scatter(partial_term(jnp.int32(0), share_rows * lax.axis_size('r...  290 us
    reduce_scatter x8, waiting for transfers between devices, reduce_cols(): lax.psum_scatter(partial_term(jnp.int32(0), share_rows * lax.axis_size('c...  228 us
    all_gather x8, waiting for transfers between devices, spread_rows(): return lax.all_gather(values, 'row', axis=0, tiled=True)  152 us
    all_gather x8, blocking collectives, spread_cols(): return lax.all_gather(values, 'col', axis=0, tiled=True)  145 us
    dot_general x20, matrix products, contract_last(): lax.dot_general(left, right, (((1,), (1,)), ((), ())), preferred_element_...  45.8 us
    unnamed x191, local copies, waits for them, and re-layouts  26.9 us
    dot_general x20, matrix products, contract_first(): lax.dot_general(left, right, (((0,), (0,)), ((), ())), preferred_element_...  25.9 us
    psum x4, blocking collectives, feature_sums(): return lax.psum((first_sum, second_sum), 'row')  25.4 us
  transfers between devices with their start and end apart: 31, of which 27 were waited for; matrix products, arithmetic and copies ran while one was open for 14% of the time, Pallas kernels for 0%

commit v1 on v0

--- a/solution.py
+++ b/solution.py
@@ -6,6 +6,27 @@
 DH = 64
 EPSILON = 1e-05
 MASKED_SCORE = -1e30
+
+
+def collect(value, axis, dim):
+    length, here, width = (lax.axis_size(axis), lax.axis_index(axis), value.shape[dim])
+    right = [(i, (i + 1) % length) for i in range(length)]
+    behind = [(i, (i - 1) % length) for i in range(length)]
+    out = jnp.zeros((*value.shape[:dim], length * width, *value.shape[dim + 1 :]), value.dtype)
+    out = lax.dynamic_update_slice_in_dim(out, value, here * width, axis=dim)
+    from_left = from_right = value
+    halfway = length // 2
+    for lap in range(1, halfway + 1):
+        from_left = lax.ppermute(from_left, axis, right)
+        out = lax.dynamic_update_slice_in_dim(
+            out, from_left, (here - lap) % length * width, axis=dim
+        )
+        if lap < length - halfway:
+            from_right = lax.ppermute(from_right, axis, behind)
+            out = lax.dynamic_update_slice_in_dim(
+                out, from_right, (here + lap) % length * width, axis=dim
+            )
+    return out
 
 
 def rotate(values, positions, rotation_sign):
@@ -46,7 +67,7 @@
 
 
 def spread_cols(values):
-    return lax.all_gather(values, "col", axis=0, tiled=True)
+    return collect(values, "col", 0)
 
 
 def spread_rows(values):

time: 1260 us -> 1210 us (0.960)
  blocking collectives: 225 us -> 79.9 us
  waiting for transfers between devices: 702 us -> 768 us
  starting transfers between devices: 17.1 us -> 57.1 us
    all_gather x8 -> x0, blocking collectives: 145 us -> none  [spread_cols(): return lax.all_gather(values, 'col', axis=0, tiled=True)]
    ppermute x0 -> x24, waiting for transfers between devices: none -> 90.5 us  [the longest x16 86.5 us: collect(): from_left = lax.ppermute(from_left, axis, right)]
    ppermute x0 -> x24, starting transfers between devices: none -> 39.5 us  [the longest x8 28.2 us: collect(): from_right = lax.ppermute(from_right, axis, behind)]
    reduce_scatter x8, waiting for transfers between devices: 290 us -> 268 us  [reduce_rows(): lax.psum_scatter(partial_term(jnp.int32(0), share_rows * lax.axis_size('r...]
    unnamed x191 -> x275, local copies, waits for them, and re-layouts: 26.9 us -> 27.3 us
  transfers between devices with their start and end apart: 31 -> 55, of which waited for: 27 -> 47; matrix products, arithmetic and copies ran while one was open for 14% -> 17% of each run, Pallas kernels for 0% -> 0%
where the time goes in v1:
time: 1210 us
  waiting for transfers between devices  768 us (63%)
  matrix products  116 us (10%)
  local copies, waits for them, and re-layouts  84.4 us (7%)
  other arithmetic  82 us (7%)
  blocking collectives  79.9 us (7%)
  starting transfers between devices  57.1 us (5%)
  between operations  17.2 us (1%)
    reduce_scatter x8, waiting for transfers between devices, reduce_rows(): lax.psum_scatter(partial_term(jnp.int32(0), share_rows * lax.axis_size('r...  268 us
    reduce_scatter x8, waiting for transfers between devices, reduce_cols(): lax.psum_scatter(partial_term(jnp.int32(0), share_rows * lax.axis_size('c...  226 us
    all_gather x8, waiting for transfers between devices, spread_rows(): return lax.all_gather(values, 'row', axis=0, tiled=True)  152 us
    ppermute x16, waiting for transfers between devices, collect(): from_left = lax.ppermute(from_left, axis, right)  86.5 us
    dot_general x20, matrix products, contract_last(): lax.dot_general(left, right, (((1,), (1,)), ((), ())), preferred_element_...  45.8 us
    ppermute x8, starting transfers between devices, collect(): from_right = lax.ppermute(from_right, axis, behind)  28.2 us
    unnamed x275, local copies, waits for them, and re-layouts  27.3 us
    dot_general x20, matrix products, contract_first(): lax.dot_general(left, right, (((0,), (0,)), ((), ())), preferred_element_...  26.9 us
  transfers between devices with their start and end apart: 55, of which 47 were waited for; matrix products, arithmetic and copies ran while one was open for 17% of the time, Pallas kernels for 0%

profile of v1, /device:TPU:0, one launch (start us, length us, event | category | flops | bytes accessed | tf_op | source)
XLA Modules:
  0.0 1205.1 jit_solution(2238311936577653710)
XLA Ops:
  12.3 8.8 gather_fusion
  39.0 7.0 all-to-all-done.1
  54.5 5.6 collective-permute-done.6
  81.1 6.8 collective-permute-done.2
  95.7 22.4 %reduce-scatter.27.cloned.1.call-done = f32[512,576]{0,1:T(8,128)} async-done(((f32[2048,576]{0,1:T(8,128)}), f32[512,576]{0,1:T(8,128)}) %reduce-scatter.27.cloned.1.call-update) | async-done | bytes 1179664 | tf_op jit(solution)/shard_map/reduce_scatter | solution.py:82
  126.6 42.1 %reduce-scatter.19.cloned.1.call-done = f32[512,576]{0,1:T(8,128)} async-done(((f32[2048,576]{0,1:T(8,128)}), f32[512,576]{0,1:T(8,128)}) %reduce-scatter.19.cloned.1.call-update) | async-done | bytes 1179664 | tf_op jit(solution)/shard_map/reduce_scatter | solution.py:82
  174.3 16.2 %all-gather.13.cloned.1.call-done = bf16[2048,384]{0,1:T(8,128)(2,1)} async-done(((bf16[512,384]{0,1:T(8,128)(2,1)}), bf16[2048,384]{0,1:T(8,128)(2,1)}) %all-gather.13.cloned.1.call-update) | async-done | bytes 1572880 | tf_op jit(solution)/shard_map/all_gather | solution.py:74
  201.5 13.3 %all_gather.34 = bf16[2048,192]{0,1:T(8,128)(2,1)S(1)} all-gather(bf16[512,192]{0,1:T(8,128)(2,1)S(1)} %pad_maximum_fusion.14), channel_id=1, replica_groups=mesh['dp'=2,'row'=4,'col'=4] {'row'}, dimensions={0}, use_global_device_ids=true | all-gather | bytes 983040 | tf_op jit(solution)/shard_map/all_gather | solution.py:74
  228.4 8.7 all_gather.31
  239.8 14.2 %reduce-scatter.29.cloned.1.call-done = f32[512,192]{0,1:T(8,128)} async-done(((f32[2048,192]{0,1:T(8,128)}), f32[512,192]{0,1:T(8,128)}) %reduce-scatter.29.cloned.1.call-update) | async-done | bytes 393232 | tf_op jit(solution)/shard_map/reduce_scatter | solution.py:95
  255.0 35.4 %reduce-scatter.21.cloned.1.call-done = f32[512,192]{0,1:T(8,128)} async-done(((f32[2048,192]{0,1:T(8,128)}), f32[512,192]{0,1:T(8,128)}) %reduce-scatter.21.cloned.1.call-update) | async-done | bytes 393232 | tf_op jit(solution)/shard_map/reduce_scatter | solution.py:95
  291.5 6.6 all-reduce.4
  302.2 5.8 collective-permute-done.3
  308.7 6.9 collective-permute-done.5
  330.3 5.4 collective-permute-done.11
  341.4 35.0 %reduce-scatter.23.cloned.1.call-done = f32[512,768]{1,0:T(8,128)} async-done(((f32[2048,768]{1,0:T(8,128)}), f32[512,768]{1,0:T(8,128)}) %reduce-scatter.23.cloned.1.call-update) | async-done | bytes 1572880 | tf_op jit(solution)/shard_map/reduce_scatter | solution.py:82
  376.4 5.5 multiply_convert_fusion.7
  382.0 55.5 %reduce-scatter.31.cloned.1.call-done = f32[512,768]{1,0:T(8,128)} async-done(((f32[2048,768]{1,0:T(8,128)}), f32[512,768]{1,0:T(8,128)}) %reduce-scatter.31.cloned.1.call-update) | async-done | bytes 1572880 | tf_op jit(solution)/shard_map/reduce_scatter | solution.py:82
  437.5 5.5 multiply_convert_fusion.6
  443.1 24.6 %all-gather.11.cloned.1.call-done = bf16[2048,768]{1,0:T(8,128)(2,1)} async-done(((bf16[512,768]{1,0:T(8,128)(2,1)}), bf16[2048,768]{1,0:T(8,128)(2,1)}) %all-gather.11.cloned.1.call-update) | async-done | bytes 3145744 | tf_op jit(solution)/shard_map/all_gather | solution.py:74
  471.9 25.7 %all-gather.15.cloned.1.call-done = bf16[2048,768]{1,0:T(8,128)(2,1)} async-done(((bf16[512,768]{1,0:T(8,128)(2,1)}), bf16[2048,768]{1,0:T(8,128)(2,1)}) %all-gather.15.cloned.1.call-update) | async-done | bytes 3145744 | tf_op jit(solution)/shard_map/all_gather | solution.py:74
  507.2 9.7 all_to_all.57
  521.3 13.9 %reduce-scatter.25.cloned.1.call-done = f32[512,192]{0,1:T(8,128)} async-done(((f32[2048,192]{0,1:T(8,128)}), f32[512,192]{0,1:T(8,128)}) %reduce-scatter.25.cloned.1.call-update) | async-done | bytes 393232 | tf_op jit(solution)/shard_map/reduce_scatter | solution.py:95
  535.2 36.5 %reduce-scatter.33.cloned.1.call-done = f32[512,192]{0,1:T(8,128)} async-done(((f32[2048,192]{0,1:T(8,128)}), f32[512,192]{0,1:T(8,128)}) %reduce-scatter.33.cloned.1.call-update) | async-done | bytes 393232 | tf_op jit(solution)/shard_map/reduce_scatter | solution.py:95
  573.1 6.5 all-reduce.3
  580.6 5.9 all-reduce.2
  590.6 5.8 collective-permute-done.12
  597.9 6.0 collective-permute-done.14
  619.8 4.9 collective-permute-done.20
  629.9 35.5 %reduce-scatter.35.cloned.1.call-done = f32[512,768]{1,0:T(8,128)} async-done(((f32[2048,768]{1,0:T(8,128)}), f32[512,768]{1,0:T(8,128)}) %reduce-scatter.35.cloned.1.call-update) | async-done | bytes 1572880 | tf_op jit(solution)/shard_map/reduce_scatter | solution.py:82
  669.0 57.3 %reduce-scatter.45.cloned.1.call-done = f32[512,768]{1,0:T(8,128)} async-done(((f32[2048,768]{1,0:T(8,128)}), f32[512,768]{1,0:T(8,128)}) %reduce-scatter.45.cloned.1.call-update) | async-done | bytes 1572880 | tf_op jit(solution)/shard_map/reduce_scatter | solution.py:82
  730.3 26.0 %all-gather.17.cloned.1.call-done = bf16[2048,768]{1,0:T(8,128)(2,1)} async-done(((bf16[512,768]{1,0:T(8,128)(2,1)}), bf16[2048,768]{1,0:T(8,128)(2,1)}) %all-gather.17.cloned.1.call-update) | async-done | bytes 3145744 | tf_op jit(solution)/shard_map/all_gather | solution.py:74
  760.6 25.7 %all-gather.21.cloned.1.call-done = bf16[2048,768]{1,0:T(8,128)(2,1)} async-done(((bf16[512,768]{1,0:T(8,128)(2,1)}), bf16[2048,768]{1,0:T(8,128)(2,1)}) %all-gather.21.cloned.1.call-update) | async-done | bytes 3145744 | tf_op jit(solution)/shard_map/all_gather | solution.py:74
  790.6 33.1 %reduce-scatter.37.cloned.1.call-done = f32[512,192]{0,1:T(8,128)} async-done(((f32[2048,192]{0,1:T(8,128)}), f32[512,192]{0,1:T(8,128)}) %reduce-scatter.37.cloned.1.call-update) | async-done | bytes 393232 | tf_op jit(solution)/shard_map/reduce_scatter | solution.py:95
  826.4 33.8 %reduce-scatter.47.cloned.1.call-done = f32[512,192]{0,1:T(8,128)} async-done(((f32[2048,192]{0,1:T(8,128)}), f32[512,192]{0,1:T(8,128)}) %reduce-scatter.47.cloned.1.call-update) | async-done | bytes 393232 | tf_op jit(solution)/shard_map/reduce_scatter | solution.py:95
  862.9 6.5 all-reduce.1
  873.5 5.8 collective-permute-done.21
  879.9 6.9 collective-permute-done.23
  899.3 5.8 collective-permute-done.17
  907.7 7.7 reduce-scatter.49.cloned.1.call-done
  933.8 12.3 %reduce-scatter.39.cloned.1.call-done = f32[512,192]{0,1:T(8,128)} async-done(((f32[2048,192]{0,1:T(8,128)}), f32[512,192]{0,1:T(8,128)}) %reduce-scatter.39.cloned.1.call-update) | async-done | bytes 393232 | tf_op jit(solution)/shard_map/reduce_scatter | solution.py:82
  991.2 16.6 %reduce-scatter.41.cloned.1.call-done = bf16[512,384]{0,1:T(8,128)(2,1)} async-done(((bf16[2048,384]{0,1:T(8,128)(2,1)}), bf16[512,384]{0,1:T(8,128)(2,1)}) %reduce-scatter.41.cloned.1.call-update) | async-done | bytes 393232 | tf_op jit(solution)/shard_map/reduce_scatter | solution.py:285
  1023.9 10.2 all-gather.23.cloned.1.call-done
  1036.8 23.4 %all-gather.19.cloned.1.call-done = bf16[2048,576]{0,1:T(8,128)(2,1)} async-done(((bf16[512,576]{0,1:T(8,128)(2,1)}), bf16[2048,576]{0,1:T(8,128)(2,1)}) %all-gather.19.cloned.1.call-update) | async-done | bytes 2359312 | tf_op jit(solution)/shard_map/all_gather | solution.py:74
  1083.5 22.8 %all-reduce = (f32[192]{0:T(256)}, f32[192]{0:T(256)}, f32[192]{0:T(256)}, f32[192]{0:T(256)}) all-reduce(f32[192]{0:T(256)S(1)} %add.440, f32[192]{0:T(256)S(1)} %add.441, f32[192]{0:T(256)S(1)} %add.442, f32[192]{0:T(256)S(1)} %add.443), channel_id=1, replica_groups=mesh['dp'=2,'row'=4,'col'=4] {'dp','col'}, use_global_device_ids=true, to_apply=%region_77.78 | all-reduce | flops 768 | bytes 6144 | tf_op jit(solution)/shard_map/psum | solution.py:306
  1116.7 23.0 %reduce-scatter.53.cloned.1.call-done = f32[512,192]{0,1:T(8,128)} async-done(((f32[2048,192]{0,1:T(8,128)}), f32[512,192]{0,1:T(8,128)}) %reduce-scatter.53.cloned.1.call-update) | async-done | bytes 393232 | tf_op jit(solution)/shard_map/reduce_scatter | solution.py:95
  1139.7 36.5 %reduce-scatter.43.cloned.1.call-done = f32[512,192]{0,1:T(8,128)} async-done(((f32[2048,192]{0,1:T(8,128)}), f32[512,192]{0,1:T(8,128)}) %reduce-scatter.43.cloned.1.call-update) | async-done | bytes 393232 | tf_op jit(solution)/shard_map/reduce_scatter | solution.py:95
  1187.2 5.8 all-to-all-done.4
  (608 shorter events, 347.0 us)
Async XLA Ops:
  21.2 8.8 all-to-all-start
  35.4 10.5 all-to-all-start.1
  38.9 79.2 %reduce-scatter.27.cloned.1.call-start = ((), (), s32[]{:S(2)}) async-start(), calls=%async_computation.29 | async-start | bytes 5898240 | tf_op jit(solution)/shard_map/reduce_scatter | solution.py:82
  50.3 9.8 collective-permute-start.6
  52.2 10.5 collective-permute-start.7
  71.7 97.0 %reduce-scatter.19.cloned.1.call-start = ((), (), s32[]{:S(2)}) async-start(), calls=%async_computation.23 | async-start | bytes 5898240 | tf_op jit(solution)/shard_map/reduce_scatter | solution.py:82
  71.8 7.9 collective-permute-start
  71.9 9.2 collective-permute-start.1
  79.7 8.2 collective-permute-start.2
  92.0 98.5 %all-gather.13.cloned.1.call-start = ((), (), s32[]{:S(2)}) async-start(), calls=%async_computation.30 | async-start | bytes 1966080 | tf_op jit(solution)/shard_map/all_gather | solution.py:74
  123.1 94.4 %all-gather.9.cloned.1.call-start = ((), (), s32[]{:S(2)}) async-start(), calls=%async_computation.24 | async-start | bytes 1966080 | tf_op jit(solution)/shard_map/all_gather | solution.py:74
  174.3 79.7 %reduce-scatter.29.cloned.1.call-start = ((), (), s32[]{:S(2)}) async-start(), calls=%async_computation.31 | async-start | bytes 1966080 | tf_op jit(solution)/shard_map/reduce_scatter | solution.py:95
  217.2 73.2 %reduce-scatter.21.cloned.1.call-start = ((), (), s32[]{:S(2)}) async-start(), calls=%async_computation.25 | async-start | bytes 1966080 | tf_op jit(solution)/shard_map/reduce_scatter | solution.py:95
  239.7 136.7 %reduce-scatter.23.cloned.1.call-start = ((), (), s32[]{:S(2)}) async-start(), calls=%async_computation.26 | async-start | bytes 7864320 | tf_op jit(solution)/shard_map/reduce_scatter | solution.py:82
  298.3 9.7 collective-permute-start.3
  298.4 10.2 collective-permute-start.4
  320.2 117.3 %reduce-scatter.31.cloned.1.call-start = ((), (), s32[]{:S(2)}) async-start(), calls=%async_computation.32 | async-start | bytes 7864320 | tf_op jit(solution)/shard_map/reduce_scatter | solution.py:82
  320.5 7.7 collective-permute-start.9
  320.6 9.7 collective-permute-start.10
  340.9 126.8 %all-gather.11.cloned.1.call-start = ((), (), s32[]{:S(2)}) async-start(), calls=%async_computation.27 | async-start | bytes 3932160 | tf_op jit(solution)/shard_map/all_gather | solution.py:74
  382.0 115.6 %all-gather.15.cloned.1.call-start = ((), (), s32[]{:S(2)}) async-start(), calls=%async_computation.33 | async-start | bytes 3932160 | tf_op jit(solution)/shard_map/all_gather | solution.py:74
  443.0 92.2 %reduce-scatter.25.cloned.1.call-start = ((), (), s32[]{:S(2)}) async-start(), calls=%async_computation.28 | async-start | bytes 1966080 | tf_op jit(solution)/shard_map/reduce_scatter | solution.py:95
  471.9 99.8 %reduce-scatter.33.cloned.1.call-start = ((), (), s32[]{:S(2)}) async-start(), calls=%async_computation.34 | async-start | bytes 1966080 | tf_op jit(solution)/shard_map/reduce_scatter | solution.py:95
  501.9 163.5 %reduce-scatter.35.cloned.1.call-start = ((), (), s32[]{:S(2)}) async-start(), calls=%async_computation.35 | async-start | bytes 7864320 | tf_op jit(solution)/shard_map/reduce_scatter | solution.py:82
  586.8 9.7 collective-permute-start.12
  587.2 10.7 collective-permute-start.13
  608.6 117.7 %reduce-scatter.45.cloned.1.call-start = ((), (), s32[]{:S(2)}) async-start(), calls=%async_computation.42 | async-start | bytes 7864320 | tf_op jit(solution)/shard_map/reduce_scatter | solution.py:82
  608.9 8.3 collective-permute-start.18
  609.0 10.8 collective-permute-start.19
  629.8 126.5 %all-gather.17.cloned.1.call-start = ((), (), s32[]{:S(2)}) async-start(), calls=%async_computation.36 | async-start | bytes 3932160 | tf_op jit(solution)/shard_map/all_gather | solution.py:74
  668.8 117.5 %all-gather.21.cloned.1.call-start = ((), (), s32[]{:S(2)}) async-start(), calls=%async_computation.43 | async-start | bytes 3932160 | tf_op jit(solution)/shard_map/all_gather | solution.py:74
  730.3 93.5 %reduce-scatter.37.cloned.1.call-start = ((), (), s32[]{:S(2)}) async-start(), calls=%async_computation.37 | async-start | bytes 1966080 | tf_op jit(solution)/shard_map/reduce_scatter | solution.py:95
  760.6 99.7 %reduce-scatter.47.cloned.1.call-start = ((), (), s32[]{:S(2)}) async-start(), calls=%async_computation.44 | async-start | bytes 1966080 | tf_op jit(solution)/shard_map/reduce_scatter | solution.py:95
  790.6 124.8 %reduce-scatter.49.cloned.1.call-start = ((), (), s32[]{:S(2)}) async-start(), calls=%async_computation.45 | async-start | bytes 1966080 | tf_op jit(solution)/shard_map/reduce_scatter | solution.py:82
  869.6 9.7 collective-permute-start.21
  869.7 10.2 collective-permute-start.22
  889.4 56.8 %reduce-scatter.39.cloned.1.call-start = ((), (), s32[]{:S(2)}) async-start(), calls=%async_computation.38 | async-start | bytes 1966080 | tf_op jit(solution)/shard_map/reduce_scatter | solution.py:82
  889.9 7.7 collective-permute-start.15
  890.2 9.0 collective-permute-start.16
  907.6 69.4 %reduce-scatter.51.cloned.1.call-start = ((), (), s32[]{:S(2)}) async-start(), calls=%async_computation.46 | async-start | bytes 1966080 | tf_op jit(solution)/shard_map/reduce_scatter | solution.py:285
  933.6 74.3 %reduce-scatter.41.cloned.1.call-start = ((), (), s32[]{:S(2)}) async-start(), calls=%async_computation.39 | async-start | bytes 1966080 | tf_op jit(solution)/shard_map/reduce_scatter | solution.py:285
  968.3 65.8 %all-gather.23.cloned.1.call-start = ((), (), s32[]{:S(2)}) async-start(), calls=%async_computation.47 | async-start | bytes 2949120 | tf_op jit(solution)/shard_map/all_gather | solution.py:74
  984.9 75.3 %all-gather.19.cloned.1.call-start = ((), (), s32[]{:S(2)}) async-start(), calls=%async_computation.40 | async-start | bytes 2949120 | tf_op jit(solution)/shard_map/all_gather | solution.py:74
  1012.2 99.3 %all-reduce.8.cloned.1.call-start = ((), (), s32[]{:S(2)}) async-start(), calls=%async_computation.49 | async-start | bytes 1867776 | tf_op jit(solution)/shard_map/psum | solution.py:301
  1063.6 76.1 %reduce-scatter.53.cloned.1.call-start = ((), (), s32[]{:S(2)}) async-start(), calls=%async_computation.48 | async-start | bytes 1966080 | tf_op jit(solution)/shard_map/reduce_scatter | solution.py:95
  1067.6 108.7 %reduce-scatter.43.cloned.1.call-start = ((), (), s32[]{:S(2)}) async-start(), calls=%async_computation.41 | async-start | bytes 1966080 | tf_op jit(solution)/shard_map/reduce_scatter | solution.py:95
  1079.9 26.5 %all-to-all-start.2 = ((bf16[2,512,192]{1,2,0:T(8,128)(2,1)}), bf16[2,512,192]{1,2,0:T(8,128)(2,1)S(1)}, u32[]{:S(2)}, u32[]{:S(2)}) async-start(bf16[2,512,192]{1,2,0:T(8,128)(2,1)} %copy.52), calls=%async_computation.10 | async-start | bytes 786432 | tf_op jit(solution)/shard_map/all_to_all | solution.py:312
  1182.9 10.1 all-to-all-start.4
  (142 other events, 3675.7 us)
Sparse Core Ops, SparseCore 0:
  71.8 46.2 reduce-scatter.26
  120.8 47.8 reduce-scatter.18
  170.8 19.6 all-gather.12
  192.5 23.8 all-gather.8
  218.6 35.3 reduce-scatter.28
  256.1 34.2 reduce-scatter.20
  320.4 56.0 reduce-scatter.22
  379.1 58.3 reduce-scatter.30
  439.1 28.5 all-gather.10
  469.0 28.5 all-gather.14
  499.9 35.2 reduce-scatter.24
  537.4 34.2 reduce-scatter.32
  608.7 56.6 reduce-scatter.34
  667.9 58.3 reduce-scatter.44
  727.7 28.5 all-gather.16
  757.7 28.5 all-gather.20
  788.5 35.2 reduce-scatter.36
  825.9 34.2 reduce-scatter.46
  889.5 25.8 reduce-scatter.48
  918.0 28.1 reduce-scatter.38
  948.7 28.2 reduce-scatter.50
  979.7 28.0 reduce-scatter.40
  1010.0 24.0 all-gather.22
  1036.1 24.0 all-gather.18
  1063.8 38.2 all-reduce.7
  1104.3 35.3 reduce-scatter.52
  1142.0 34.2 reduce-scatter.42
